TPU v7x, 32 devices: a whole 2x2x4 slice. The times are simulated.
32 devices in a mesh: ctx: 8 (over z, y), shard: 4 (over x, core).
Axes of the slice: x: 2, y: 2, z: 4, core: 2. Of those that a mesh axis runs over, the one named last changes fastest.
Arguments:
- block_in: bfloat16 [1024, 1024], P('ctx'), may hold values from -6 to 6
- attn_gain: float32 [1024], replicated, may hold values from 0.5 to 1.5
- q_weight: bfloat16 [1024, 1024], P(None, 'shard'), may hold values from -0.1875 to 0.1875
- k_weight: bfloat16 [1024, 512], P(None, 'shard'), may hold values from -0.1875 to 0.1875
- v_weight: bfloat16 [1024, 512], P(None, 'shard'), may hold values from -0.1875 to 0.1875
- o_weight: bfloat16 [1024, 1024], P('shard'), may hold values from -1.5 to 1.5
- moe_gain: float32 [1024], replicated, may hold values from 0.5 to 1.5
- router_weight: bfloat16 [1024, 16], replicated, may hold values from -0.1875 to 0.1875
- expert_gate: bfloat16 [16, 1024, 512], P('shard'), may hold values from -0.1875 to 0.1875
- expert_up: bfloat16 [16, 1024, 512], P('shard'), may hold values from -0.1875 to 0.1875
- expert_down: bfloat16 [16, 512, 1024], P('shard'), may hold values from -0.5 to 0.5
- routes: int32 [1024, 8], P('ctx'), may hold values from 0 to 15, all different within a row; in each aligned block of 128 rows (0 to 127, 128 to 255, ...) at most 112 rows name the same one
- out_grad: float32 [1024, 1024], P('ctx'), may hold values from -6 to 6
Outputs:
- block_out: float32 [1024, 1024], P('ctx')
- in_grad: float32 [1024, 1024], P('ctx')
- attn_gain_grad: float32 [1024], P('ctx')
- q_weight_grad: float32 [1024, 1024], P('ctx', 'shard')
- k_weight_grad: float32 [1024, 512], P('ctx', 'shard')
- v_weight_grad: float32 [1024, 512], P('ctx', 'shard')
- o_weight_grad: float32 [1024, 1024], P('shard', 'ctx')
- moe_gain_grad: float32 [1024], P('ctx')
- router_grad: float32 [1024, 16], P('ctx')
- gate_grad: float32 [16, 1024, 512], P('shard', 'ctx')
- up_grad: float32 [16, 1024, 512], P('shard', 'ctx')
- down_grad: float32 [16, 512, 1024], P('shard', None, 'ctx')
Inputs may be any that keep to these rules, and one draw needn't show every extreme that they name: `routes`: each row names 8 different experts; in each aligned block of 128 rows (128; a device may hold several) no expert is named by more than 112 rows.
All inputs are finite; a program needn't handle non-finite values.
Results may differ from a plain program's by a relative error of at most 0.015.
Values may be sent and summed in bfloat16 or wider, within the bound.
No kernel may reach another device: no remote copies, remote signals or barrier semaphores. Data moves between devices by JAX's collectives and lax.ppermute only.
A program may use at most 128 MiB of HBM per device.

v0:
```python
import math
import jax
import jax.numpy as jnp
from jax import lax
from jax.sharding import PartitionSpec as P

HD = 64
CAP = 112
NORM_EPS = 1e-06
ROPE_BASE = 10000.0


def rope_tables(positions, head_width):
    half_width = head_width // 2
    freq_steps = jnp.arange(half_width, dtype=jnp.float32) * (2.0 / head_width)
    inv_freq = jnp.exp(-math.log(ROPE_BASE) * freq_steps)
    angles = positions.astype(jnp.float32)[:, None] * inv_freq[None, :]
    cos_tab = jnp.concatenate([jnp.cos(angles), jnp.cos(angles)], axis=1)
    sin_tab = jnp.concatenate([jnp.sin(angles), jnp.sin(angles)], axis=1)
    return (cos_tab, sin_tab)


def rotate_heads(head_vals, cos_tab, sin_tab):
    half_width = head_vals.shape[-1] // 2
    turned = jnp.concatenate([-head_vals[..., half_width:], head_vals[..., :half_width]], axis=-1)
    return head_vals * cos_tab[:, None, :] + turned * sin_tab[:, None, :]


def unrotate_heads(head_grads, cos_tab, sin_tab):
    half_width = head_grads.shape[-1] // 2
    scaled = head_grads * sin_tab[:, None, :]
    back = jnp.concatenate([scaled[..., half_width:], -scaled[..., :half_width]], axis=-1)
    return head_grads * cos_tab[:, None, :] + back


def rms_forward(inputs, gain):
    inverse = lax.rsqrt(jnp.mean(inputs * inputs, axis=-1, keepdims=True) + NORM_EPS)
    return (inputs * inverse * gain, inverse)


def rms_backward(inputs, inverse, gain, grads):
    scaled = grads * gain
    inner = jnp.mean(scaled * inputs, axis=-1, keepdims=True)
    d_inputs = inverse * scaled - inputs * inverse * inverse * inverse * inner
    d_gain = jnp.sum(grads * inputs * inverse, axis=0)
    return (d_inputs, d_gain)


def slot_tables(routes, n_experts):
    expert_ids = jnp.arange(n_experts, dtype=jnp.int32)
    expert_hits = jnp.sum(
        (routes[:, :, None] == expert_ids[None, None, :]).astype(jnp.int32), axis=1
    )
    earlier_hits = jnp.cumsum(expert_hits, axis=0) - expert_hits
    slot_ids = jnp.take_along_axis(earlier_hits, routes, axis=1)
    return (expert_hits, earlier_hits, slot_ids)


def spread_to_experts(values_tk, routes, n_experts):
    expert_ids = jnp.arange(n_experts, dtype=jnp.int32)
    return jnp.sum(
        jnp.where(routes[:, :, None] == expert_ids[None, None, :], values_tk[:, :, None], 0.0),
        axis=1,
    )


def slot_rows(expert_hits, earlier_hits, weight_table, first_expert, expert_count, capacity):
    local_hits = lax.dynamic_slice_in_dim(expert_hits, first_expert, expert_count, 1).T
    local_earlier = lax.dynamic_slice_in_dim(earlier_hits, first_expert, expert_count, 1).T
    local_weight = lax.dynamic_slice_in_dim(weight_table, first_expert, expert_count, 1).T
    slot_range = jnp.arange(capacity, dtype=jnp.int32)
    matched = (local_hits[:, None, :] > 0) & (
        local_earlier[:, None, :] == slot_range[None, :, None]
    )
    row_range = jnp.arange(expert_hits.shape[0], dtype=jnp.int32)
    row_ids = jnp.sum(jnp.where(matched, row_range[None, None, :], 0), axis=2)
    row_valid = jnp.any(matched, axis=2)
    slot_weight = jnp.sum(jnp.where(matched, local_weight[:, None, :], 0.0), axis=2)
    return (row_ids, row_valid, slot_weight)


def body(
    block_in,
    attn_gain,
    q_weight,
    k_weight,
    v_weight,
    o_weight,
    moe_gain,
    router_weight,
    expert_gate,
    expert_up,
    expert_down,
    routes,
    out_grad,
):
    row_count = block_in.shape[0]
    model_width = block_in.shape[1]
    seq_len = row_count * lax.axis_size("ctx")
    q_local = q_weight.shape[1] // HD
    kv_local = k_weight.shape[1] // HD
    group = q_local // kv_local
    scale = HD ** (-0.5)
    key_block = math.gcd(512, seq_len)
    first_row = lax.axis_index("ctx") * row_count
    blocks_needed = (first_row + row_count + key_block - 1) // key_block
    positions = first_row + jnp.arange(row_count, dtype=jnp.int32)
    cos_tab, sin_tab = rope_tables(positions, HD)
    resid_in = block_in.astype(jnp.float32)
    normed_one, inverse_one = rms_forward(resid_in, attn_gain)
    normed_one = normed_one.astype(jnp.bfloat16)
    query_rot = rotate_heads(
        jnp.dot(normed_one, q_weight, preferred_element_type=jnp.float32).reshape(
            row_count, q_local, HD
        ),
        cos_tab,
        sin_tab,
    ).astype(jnp.bfloat16)
    query_groups = query_rot.reshape(row_count, kv_local, group, HD)
    key_rot = (
        rotate_heads(
            jnp.dot(normed_one, k_weight, preferred_element_type=jnp.float32).reshape(
                row_count, kv_local, HD
            ),
            cos_tab,
            sin_tab,
        )
        .astype(jnp.bfloat16)
        .reshape(row_count, kv_local * HD)
    )
    value_proj = jnp.dot(normed_one, v_weight, preferred_element_type=jnp.float32).astype(
        jnp.bfloat16
    )

    def masked_scores(key_piece, key_start):
        piece_len = key_piece.shape[0]
        raw = (
            jnp.einsum(
                "tngd,jnd->ngtj",
                query_groups,
                key_piece.reshape(piece_len, kv_local, HD),
                preferred_element_type=jnp.float32,
            )
            * scale
        )
        key_pos = key_start + jnp.arange(piece_len, dtype=jnp.int32)
        allowed = key_pos[None, :] <= positions[:, None]
        return jnp.where(allowed[None, None], raw, -jnp.inf)

    running_top = jnp.full((kv_local, group, row_count), -1e30, jnp.float32)
    scores = masked_scores(lax.all_gather(key_rot, "ctx", axis=0, tiled=True), jnp.int32(0))
    new_top = jnp.maximum(running_top, jnp.max(scores, axis=-1))
    new_total = jnp.sum(jnp.exp(scores - new_top[..., None]), axis=-1)
    log_total = new_top + jnp.log(new_total)
    key_piece = lax.all_gather(key_rot, "ctx", axis=0, tiled=True)
    value_piece = lax.all_gather(value_proj, "ctx", axis=0, tiled=True)
    scores = masked_scores(key_piece, jnp.int32(0))
    probs = jnp.exp(scores - log_total[..., None]).astype(jnp.bfloat16)
    piece_len = value_piece.shape[0]
    running_acc = jnp.einsum(
        "ngtj,jnd->ngtd",
        probs,
        value_piece.reshape(piece_len, kv_local, HD),
        preferred_element_type=jnp.float32,
    )
    heads_out = (
        running_acc.transpose(2, 0, 1, 3).reshape(row_count, q_local * HD).astype(jnp.bfloat16)
    )
    resid_mid = resid_in + lax.psum(
        jnp.dot(heads_out, o_weight, preferred_element_type=jnp.float32), "shard"
    )
    normed_two, inverse_two = rms_forward(resid_mid, moe_gain)
    normed_two = normed_two.astype(jnp.bfloat16)
    logits = jnp.dot(normed_two, router_weight, preferred_element_type=jnp.float32)
    gate = jax.nn.softmax(jnp.take_along_axis(logits, routes, axis=1), axis=-1)
    local_count = expert_gate.shape[0]
    n_experts = local_count * lax.axis_size("shard")
    first_expert = lax.axis_index("shard") * local_count
    expert_hits, earlier_hits, slot_ids = slot_tables(routes, n_experts)
    gate_table = spread_to_experts(gate, routes, n_experts)
    row_ids, row_valid, slot_weight = slot_rows(
        expert_hits, earlier_hits, gate_table, first_expert, local_count, CAP
    )
    buffer = jnp.where(row_valid[..., None], normed_two[row_ids], jnp.zeros((), jnp.bfloat16))
    pre_gate = jnp.einsum("ecd,edf->ecf", buffer, expert_gate, preferred_element_type=jnp.float32)
    pre_up = jnp.einsum("ecd,edf->ecf", buffer, expert_up, preferred_element_type=jnp.float32)
    sig_gate = jax.nn.sigmoid(pre_gate)
    hidden = (pre_gate * sig_gate * pre_up).astype(jnp.bfloat16)
    expert_out = jnp.einsum("ecf,efd->ecd", hidden, expert_down, preferred_element_type=jnp.float32)
    is_local = (routes >= first_expert) & (routes < first_expert + local_count)
    flat_ids = jnp.where(is_local, (routes - first_expert) * CAP + slot_ids, 0)
    picked = expert_out.reshape(local_count * CAP, model_width)[flat_ids]
    moe_part = jnp.sum(jnp.where(is_local, gate, 0.0)[..., None] * picked, axis=1)
    d_gate_part = jnp.where(is_local, jnp.sum(picked * out_grad[:, None, :], axis=-1), 0.0)
    block_out = resid_mid + lax.psum(moe_part.astype(jnp.bfloat16), "shard").astype(jnp.float32)
    d_expert_out = (jnp.where(row_valid, slot_weight, 0.0)[..., None] * out_grad[row_ids]).astype(
        jnp.bfloat16
    )
    d_hidden = jnp.einsum(
        "ecd,efd->ecf", d_expert_out, expert_down, preferred_element_type=jnp.float32
    )
    down_part = jnp.einsum("ecf,ecd->efd", hidden, d_expert_out, preferred_element_type=jnp.float32)
    d_silu = sig_gate * (1.0 + pre_gate * (1.0 - sig_gate))
    d_pre_gate = (d_hidden * pre_up * d_silu).astype(jnp.bfloat16)
    d_pre_up = (d_hidden * pre_gate * sig_gate).astype(jnp.bfloat16)
    gate_part = jnp.einsum("ecd,ecf->edf", buffer, d_pre_gate, preferred_element_type=jnp.float32)
    up_part = jnp.einsum("ecd,ecf->edf", buffer, d_pre_up, preferred_element_type=jnp.float32)
    d_buffer = jnp.einsum(
        "ecf,edf->ecd", d_pre_gate, expert_gate, preferred_element_type=jnp.float32
    ) + jnp.einsum("ecf,edf->ecd", d_pre_up, expert_up, preferred_element_type=jnp.float32)
    d_normed_part = jnp.sum(
        jnp.where(
            is_local[..., None], d_buffer.reshape(local_count * CAP, model_width)[flat_ids], 0.0
        ),
        axis=1,
    )
    d_normed_exp, d_gate = lax.psum((d_normed_part, d_gate_part), "shard")
    d_chosen = gate * (d_gate - jnp.sum(gate * d_gate, axis=-1, keepdims=True))
    d_logits = spread_to_experts(d_chosen, routes, n_experts)
    router_f = router_weight.astype(jnp.float32)
    d_normed_two = d_normed_exp + jnp.dot(d_logits, router_f.T, precision=lax.Precision.HIGHEST)
    router_part = jnp.dot(
        normed_two.astype(jnp.float32).T, d_logits, precision=lax.Precision.HIGHEST
    )
    d_resid_norm, moe_gain_part = rms_backward(resid_mid, inverse_two, moe_gain, d_normed_two)
    d_resid_mid = out_grad + d_resid_norm
    d_mid_b = d_resid_mid.astype(jnp.bfloat16)
    o_part = jnp.dot(heads_out.T, d_mid_b, preferred_element_type=jnp.float32)
    d_heads = jnp.dot(d_mid_b, o_weight.T, preferred_element_type=jnp.float32).astype(jnp.bfloat16)
    d_head_groups = d_heads.reshape(row_count, kv_local, group, HD)
    delta = jnp.sum(
        d_heads.astype(jnp.float32).reshape(row_count, kv_local, group, HD)
        * heads_out.astype(jnp.float32).reshape(row_count, kv_local, group, HD),
        axis=-1,
    ).transpose(1, 2, 0)
    keys_back, values_back = (
        lax.all_gather(key_rot, "ctx", axis=0, tiled=True),
        lax.all_gather(value_proj, "ctx", axis=0, tiled=True),
    )

    def key_step(block_idx, carry):
        d_query_acc, d_key_term, d_value_term = carry
        key_start = block_idx * key_block
        key_piece = lax.dynamic_slice_in_dim(keys_back, key_start, key_block, 0)
        value_piece = lax.dynamic_slice_in_dim(values_back, key_start, key_block, 0)
        scores = masked_scores(key_piece, key_start)
        probs = jnp.exp(scores - log_total[..., None])
        key_heads = key_piece.reshape(key_block, kv_local, HD)
        value_heads = value_piece.reshape(key_block, kv_local, HD)
        d_probs = jnp.einsum(
            "tngd,jnd->ngtj", d_head_groups, value_heads, preferred_element_type=jnp.float32
        )
        d_scores = (probs * (d_probs - delta[..., None])).astype(jnp.bfloat16)
        d_query_acc = d_query_acc + scale * jnp.einsum(
            "ngtj,jnd->tngd", d_scores, key_heads, preferred_element_type=jnp.float32
        )
        d_key_blk = scale * jnp.einsum(
            "ngtj,tngd->jnd", d_scores, query_groups, preferred_element_type=jnp.float32
        )
        d_value_blk = jnp.einsum(
            "ngtj,tngd->jnd",
            probs.astype(jnp.bfloat16),
            d_head_groups,
            preferred_element_type=jnp.float32,
        )
        d_key_term = lax.dynamic_update_slice_in_dim(
            d_key_term, d_key_blk.reshape(key_block, kv_local * HD), key_start, 0
        )
        d_value_term = lax.dynamic_update_slice_in_dim(
            d_value_term, d_value_blk.reshape(key_block, kv_local * HD), key_start, 0
        )
        return (d_query_acc, d_key_term, d_value_term)

    zero_terms = jnp.zeros((seq_len, kv_local * HD), jnp.float32)
    d_query_acc, d_key_term, d_value_term = lax.fori_loop(
        0,
        blocks_needed,
        key_step,
        (jnp.zeros((row_count, kv_local, group, HD), jnp.float32), zero_terms, zero_terms),
    )
    d_key_own, d_value_own = (
        lax.psum_scatter(d_key_term, "ctx", scatter_dimension=0, tiled=True),
        lax.psum_scatter(d_value_term, "ctx", scatter_dimension=0, tiled=True),
    )
    d_query = (
        unrotate_heads(d_query_acc.reshape(row_count, q_local, HD), cos_tab, sin_tab)
        .astype(jnp.bfloat16)
        .reshape(row_count, q_local * HD)
    )
    d_key = (
        unrotate_heads(d_key_own.reshape(row_count, kv_local, HD), cos_tab, sin_tab)
        .astype(jnp.bfloat16)
        .reshape(row_count, kv_local * HD)
    )
    d_value = d_value_own.astype(jnp.bfloat16)
    q_part = jnp.dot(normed_one.T, d_query, preferred_element_type=jnp.float32)
    k_part = jnp.dot(normed_one.T, d_key, preferred_element_type=jnp.float32)
    v_part = jnp.dot(normed_one.T, d_value, preferred_element_type=jnp.float32)
    d_normed_part_one = (
        jnp.dot(d_query, q_weight.T, preferred_element_type=jnp.float32)
        + jnp.dot(d_key, k_weight.T, preferred_element_type=jnp.float32)
        + jnp.dot(d_value, v_weight.T, preferred_element_type=jnp.float32)
    )
    d_normed_one = lax.psum(d_normed_part_one, "shard")
    d_resid_first, attn_gain_part = rms_backward(resid_in, inverse_one, attn_gain, d_normed_one)
    in_grad = d_resid_mid + d_resid_first
    (
        attn_gain_grad,
        q_weight_grad,
        k_weight_grad,
        v_weight_grad,
        o_weight_grad,
        moe_gain_grad,
        router_grad,
        gate_grad,
        up_grad,
        down_grad,
    ) = (
        lax.psum_scatter(attn_gain_part, "ctx", scatter_dimension=0, tiled=True),
        lax.psum_scatter(q_part, "ctx", scatter_dimension=0, tiled=True),
        lax.psum_scatter(k_part, "ctx", scatter_dimension=0, tiled=True),
        lax.psum_scatter(v_part, "ctx", scatter_dimension=0, tiled=True),
        lax.psum_scatter(o_part, "ctx", scatter_dimension=1, tiled=True),
        lax.psum_scatter(moe_gain_part, "ctx", scatter_dimension=0, tiled=True),
        lax.psum_scatter(router_part, "ctx", scatter_dimension=0, tiled=True),
        lax.psum_scatter(gate_part, "ctx", scatter_dimension=1, tiled=True),
        lax.psum_scatter(up_part, "ctx", scatter_dimension=1, tiled=True),
        lax.psum_scatter(down_part, "ctx", scatter_dimension=2, tiled=True),
    )
    return (
        block_out,
        in_grad,
        attn_gain_grad,
        q_weight_grad,
        k_weight_grad,
        v_weight_grad,
        o_weight_grad,
        moe_gain_grad,
        router_grad,
        gate_grad,
        up_grad,
        down_grad,
    )


def solution(mesh):
    in_specs = (
        P("ctx", None),
        P(),
        P(None, "shard"),
        P(None, "shard"),
        P(None, "shard"),
        P("shard", None),
        P(),
        P(),
        P("shard", None, None),
        P("shard", None, None),
        P("shard", None, None),
        P("ctx", None),
        P("ctx", None),
    )
    out_specs = (
        P("ctx", None),
        P("ctx", None),
        P("ctx"),
        P("ctx", "shard"),
        P("ctx", "shard"),
        P("ctx", "shard"),
        P("shard", "ctx"),
        P("ctx"),
        P("ctx", None),
        P("shard", "ctx", None),
        P("shard", "ctx", None),
        P("shard", None, "ctx"),
    )
    return jax.shard_map(body, mesh=mesh, in_specs=in_specs, out_specs=out_specs, check_vma=False)
```

profile of v0, /device:TPU:0, one launch (start us, length us, event | category | flops | bytes accessed | tf_op | source)
XLA Modules:
  0.0 1194.1 jit_solution(7015718147966698272)
XLA Ops:
  13.0 28.3 %all_gather.4 = bf16[1024,128]{0,1:T(8,128)(2,1)S(1)} all-gather(bf16[128,128]{0,1:T(8,128)(2,1)S(1)} %fusion.48), channel_id=1, replica_groups=mesh['ctx'=8,'shard'=4] {'ctx'}, dimensions={0}, use_global_device_ids=true | all-gather | bytes 294912 | tf_op jit(solution)/shard_map/all_gather | solution.py:155
  41.3 30.8 %all_gather.10 = bf16[1024,128]{1,0:T(8,128)(2,1)S(1)} all-gather(bf16[128,128]{1,0:T(8,128)(2,1)S(1)} %convolution_convert_fusion.2), channel_id=1, replica_groups=mesh['ctx'=8,'shard'=4] {'ctx'}, dimensions={0}, use_global_device_ids=true | all-gather | bytes 294912 | tf_op jit(solution)/shard_map/all_gather | solution.py:156
  75.7 7.1 gather_fusion.5
  85.8 21.8 %all-reduce.8.cloned.1.call-done = f32[128,1024]{1,0:T(8,128)} async-done(((f32[128,1024]{1,0:T(8,128)}), f32[128,1024]{1,0:T(8,128)}) %all-reduce.8.cloned.1.call-update) | async-done | bytes 524304 | tf_op jit(solution)/shard_map/psum | solution.py:169
  112.0 7.0 gather_fusion.4
  128.1 5.4 gather_fusion.1
  133.6 4.6 fusion.15
  140.4 5.9 psum.38
  157.0 5.4 gather_fusion.3
  167.6 32.7 %all-reduce.12.cloned.1.call-done = f32[128,1024]{1,0:T(8,128)} async-done(((f32[128,1024]{1,0:T(8,128)}), f32[128,1024]{1,0:T(8,128)}) %all-reduce.12.cloned.1.call-update) | async-done | bytes 524304 | tf_op jit(solution)/shard_map/psum | solution.py:217
  203.2 31.4 %all-reduce.10.cloned.1.call-done = bf16[128,1024]{1,0:T(8,128)(2,1)} async-done(((bf16[128,1024]{1,0:T(8,128)(2,1)}), bf16[128,1024]{1,0:T(8,128)(2,1)}) %all-reduce.10.cloned.1.call-update) | async-done | bytes 262160 | tf_op jit(solution)/shard_map/psum | solution.py:195
  242.8 64.4 %reduce-scatter.11.cloned.1.call-done = f32[128,128]{0,1:T(8,128)} async-done(((f32[1024,128]{0,1:T(8,128)}), f32[128,128]{0,1:T(8,128)}) %reduce-scatter.11.cloned.1.call-update) | async-done | bytes 65552 | tf_op jit(solution)/shard_map/reduce_scatter | solution.py:282
  310.2 62.2 %reduce-scatter.13.cloned.1.call-done = f32[128,128]{0,1:T(8,128)} async-done(((f32[1024,128]{0,1:T(8,128)}), f32[128,128]{0,1:T(8,128)}) %reduce-scatter.13.cloned.1.call-update) | async-done | bytes 65552 | tf_op jit(solution)/shard_map/reduce_scatter | solution.py:283
  380.7 6.0 fusion.37
  400.1 7.4 all-reduce.14.cloned.1.call-done
  408.7 21.6 %all-reduce.2 = (f32[1024]{0:T(1024)S(1)}, f32[1024]{0:T(1024)S(1)}) all-reduce(f32[1024]{0:T(1024)S(1)} %get-tuple-element.184, f32[1024]{0:T(1024)S(1)} %copy-done.46), channel_id=4, replica_groups=mesh['ctx'=8,'shard'=4] {'ctx'}, use_global_device_ids=true, to_apply=%region_30.31.clone | all-reduce | flops 2048 | bytes 16384
  433.6 31.6 %reduce-scatter.23.cloned.1.call-done = f32[128,16]{0,1:T(8,128)} async-done(((f32[1024,16]{0,1:T(8,128)}), f32[128,16]{0,1:T(8,128)}) %reduce-scatter.23.cloned.1.call-update) | async-done | bytes 8208 | tf_op jit(solution)/shard_map/reduce_scatter | solution.py:325
  465.3 67.3 %reduce-scatter.21.cloned.1.call-done = f32[256,128]{1,0:T(8,128)} async-done(((f32[256,1024]{1,0:T(8,128)}), f32[256,128]{1,0:T(8,128)}) %reduce-scatter.21.cloned.1.call-update) | async-done | bytes 131088 | tf_op jit(solution)/shard_map/reduce_scatter | solution.py:323
  532.6 64.9 %reduce-scatter.19.cloned.1.call-done = f32[128,128]{1,0:T(8,128)} async-done(((f32[1024,128]{1,0:T(8,128)}), f32[128,128]{1,0:T(8,128)}) %reduce-scatter.19.cloned.1.call-update) | async-done | bytes 65552 | tf_op jit(solution)/shard_map/reduce_scatter | solution.py:322
  597.4 65.0 %reduce-scatter.17.cloned.1.call-done = f32[128,128]{1,0:T(8,128)} async-done(((f32[1024,128]{1,0:T(8,128)}), f32[128,128]{1,0:T(8,128)}) %reduce-scatter.17.cloned.1.call-update) | async-done | bytes 65552 | tf_op jit(solution)/shard_map/reduce_scatter | solution.py:321
  662.5 66.5 %reduce-scatter.15.cloned.1.call-done = f32[128,256]{1,0:T(8,128)} async-done(((f32[1024,256]{1,0:T(8,128)}), f32[128,256]{1,0:T(8,128)}) %reduce-scatter.15.cloned.1.call-update) | async-done | bytes 131088 | tf_op jit(solution)/shard_map/reduce_scatter | solution.py:320
  728.9 153.0 %reduce-scatter.29.cloned.1.call-done = f32[4,512,128]{2,1,0:T(8,128)} async-done(((f32[4,512,1024]{2,1,0:T(8,128)}), f32[4,512,128]{2,1,0:T(8,128)}) %reduce-scatter.29.cloned.1.call-update) | async-done | bytes 1048592 | tf_op jit(solution)/shard_map/reduce_scatter | solution.py:328
  881.9 152.7 %reduce-scatter.27.cloned.1.call-done = f32[4,128,512]{2,1,0:T(8,128)} async-done(((f32[4,1024,512]{2,1,0:T(8,128)}), f32[4,128,512]{2,1,0:T(8,128)}) %reduce-scatter.27.cloned.1.call-update) | async-done | bytes 1048592 | tf_op jit(solution)/shard_map/reduce_scatter | solution.py:327
  1034.6 153.0 %reduce-scatter.25.cloned.1.call-done = f32[4,128,512]{2,1,0:T(8,128)} async-done(((f32[4,1024,512]{2,1,0:T(8,128)}), f32[4,128,512]{2,1,0:T(8,128)}) %reduce-scatter.25.cloned.1.call-update) | async-done | bytes 1048592 | tf_op jit(solution)/shard_map/reduce_scatter | solution.py:326
  (257 shorter events, 85.3 us)
Async XLA Ops:
  7.2 66.5 %copy-start = (bf16[256,1024]{1,0:T(8,128)(2,1)S(1)}, bf16[256,1024]{1,0:T(8,128)(2,1)}, u32[]{:S(2)}) copy-start(bf16[256,1024]{1,0:T(8,128)(2,1)} %param.20) | copy-start | bytes 1572868
  7.2 100.4 %all-reduce.8.cloned.1.call-start = ((), (), s32[]{:S(2)}) async-start(), calls=%async_computation.10 | async-start | bytes 1048576 | tf_op jit(solution)/shard_map/psum | solution.py:169
  13.0 60.7 %copy-start.28 = (f32[128,64]{0,1:T(8,128)}, f32[128,64]{0,1:T(8,128)S(1)}, u32[]{:S(2)}) copy-start(f32[128,64]{0,1:T(8,128)S(1)} %get-tuple-element.243) | copy-start | bytes 98308
  13.0 60.7 %copy-start.30 = (f32[128,64]{0,1:T(8,128)}, f32[128,64]{0,1:T(8,128)S(1)}, u32[]{:S(2)}) copy-start(f32[128,64]{0,1:T(8,128)S(1)} %get-tuple-element.242) | copy-start | bytes 98308
  74.8 125.5 %all-reduce.12.cloned.1.call-start = ((), (), s32[]{:S(2)}) async-start(), calls=%async_computation.12 | async-start | bytes 1048576 | tf_op jit(solution)/shard_map/psum | solution.py:217
  85.8 38.3 %copy-start.41 = (pred[4,112]{1,0:T(4,128)(4,1)}, pred[4,112]{1,0:T(4,128)(4,1)S(1)}, u32[]{:S(2)}) copy-start(pred[4,112]{1,0:T(4,128)(4,1)S(1)} %fusion.40) | copy-start | bytes 1348
  166.7 72.2 %copy-start.11 = (bf16[1024,128]{0,1:T(8,128)(2,1)S(1)}, bf16[1024,128]{0,1:T(8,128)(2,1)}, u32[]{:S(2)}) copy-start(bf16[1024,128]{0,1:T(8,128)(2,1)} %copy-done.10) | copy-start | bytes 786436
  166.7 72.2 %copy-start.13 = (bf16[1024,128]{0,1:T(8,128)(2,1)S(1)}, bf16[1024,128]{0,1:T(8,128)(2,1)}, u32[]{:S(2)}) copy-start(bf16[1024,128]{0,1:T(8,128)(2,1)} %copy-done.12) | copy-start | bytes 786436
  166.7 72.2 %copy-start.52 = (f32[2,2,128]{2,1,0:T(2,128)S(1)}, f32[2,2,128]{2,1,0:T(2,128)}, u32[]{:S(2)}) copy-start(f32[2,2,128]{2,1,0:T(2,128)} %copy-done.51) | copy-start | bytes 6148
  166.8 67.9 %all-reduce.10.cloned.1.call-start = ((), (), s32[]{:S(2)}) async-start(), calls=%async_computation.11 | async-start | bytes 524288 | tf_op jit(solution)/shard_map/psum | solution.py:195
  167.5 139.8 %reduce-scatter.11.cloned.1.call-start = ((), (), s32[]{:S(2)}) async-start(), calls=%async_computation.13 | async-start | bytes 589824 | tf_op jit(solution)/shard_map/reduce_scatter | solution.py:282
  241.8 130.6 %copy-start.32 = (bf16[1024,128]{1,0:T(8,128)(2,1)S(1)}, bf16[1024,128]{1,0:T(8,128)(2,1)}, u32[]{:S(2)}) copy-start(bf16[1024,128]{1,0:T(8,128)(2,1)} %param.19) | copy-start | bytes 786436
  241.9 130.6 %reduce-scatter.13.cloned.1.call-start = ((), (), s32[]{:S(2)}) async-start(), calls=%async_computation.14 | async-start | bytes 589824 | tf_op jit(solution)/shard_map/reduce_scatter | solution.py:283
  242.0 134.8 %copy-start.34 = (f32[1024]{0:T(1024)S(1)}, f32[1024]{0:T(1024)}, u32[]{:S(2)}) copy-start(f32[1024]{0:T(1024)} %param.16) | copy-start | bytes 12292
  242.0 134.8 %copy-start.45 = (f32[128]{0:T(128)S(1)}, f32[128]{0:T(128)}, u32[]{:S(2)}) copy-start(f32[128]{0:T(128)} %copy-done.44) | copy-start | bytes 1540
  242.5 165.1 %all-reduce.14.cloned.1.call-start = ((), (), s32[]{:S(2)}) async-start(), calls=%async_computation.15 | async-start | bytes 1048576 | tf_op jit(solution)/shard_map/psum | solution.py:304
  374.5 90.8 %reduce-scatter.23.cloned.1.call-start = ((), (), s32[]{:S(2)}) async-start(), calls=%async_computation.20 | async-start | bytes 73728 | tf_op jit(solution)/shard_map/reduce_scatter | solution.py:325
  375.4 157.2 %reduce-scatter.21.cloned.1.call-start = ((), (), s32[]{:S(2)}) async-start(), calls=%async_computation.19 | async-start | bytes 1179648 | tf_op jit(solution)/shard_map/reduce_scatter | solution.py:323
  376.8 220.7 %reduce-scatter.19.cloned.1.call-start = ((), (), s32[]{:S(2)}) async-start(), calls=%async_computation.18 | async-start | bytes 589824 | tf_op jit(solution)/shard_map/reduce_scatter | solution.py:322
  378.0 284.5 %reduce-scatter.17.cloned.1.call-start = ((), (), s32[]{:S(2)}) async-start(), calls=%async_computation.17 | async-start | bytes 589824 | tf_op jit(solution)/shard_map/reduce_scatter | solution.py:321
  379.2 349.7 %reduce-scatter.15.cloned.1.call-start = ((), (), s32[]{:S(2)}) async-start(), calls=%async_computation.16 | async-start | bytes 1179648 | tf_op jit(solution)/shard_map/reduce_scatter | solution.py:320
  380.6 501.3 %reduce-scatter.29.cloned.1.call-start = ((), (), s32[]{:S(2)}) async-start(), calls=%async_computation.23 | async-start | bytes 9437184 | tf_op jit(solution)/shard_map/reduce_scatter | solution.py:328
  386.8 647.8 %reduce-scatter.27.cloned.1.call-start = ((), (), s32[]{:S(2)}) async-start(), calls=%async_computation.22 | async-start | bytes 9437184 | tf_op jit(solution)/shard_map/reduce_scatter | solution.py:327
  392.7 794.9 %reduce-scatter.25.cloned.1.call-start = ((), (), s32[]{:S(2)}) async-start(), calls=%async_computation.21 | async-start | bytes 9437184 | tf_op jit(solution)/shard_map/reduce_scatter | solution.py:326
  (46 other events, 415.3 us)
Sparse Core Ops, SparseCore 0:
  74.9 32.6 all-reduce.7
  166.9 33.3 all-reduce.11
  202.6 31.9 all-reduce.9
  242.0 65.2 reduce-scatter.10
  311.0 61.3 reduce-scatter.12
  375.3 32.1 all-reduce.13
  411.5 53.6 reduce-scatter.22
  469.6 62.9 reduce-scatter.20
  536.5 60.8 reduce-scatter.18
  601.6 60.8 reduce-scatter.16
  666.4 62.4 reduce-scatter.14
  733.4 148.4 reduce-scatter.28
  886.1 148.4 reduce-scatter.26
  1039.1 148.4 reduce-scatter.24
where the time goes:
time: 1200 us; the launch traced here: 1190 us
  waiting for transfers between devices  975 us (81%)
  blocking collectives  86.6 us (7%)
  matrix products  48.7 us (4%)
  local copies, waits for them, and re-layouts  44 us (4%)
  other arithmetic  23.5 us (2%)
  between operations  15.5 us (1%)
    reduce_scatter x1, waiting for transfers between devices, body(): lax.psum_scatter(down_part, 'ctx', scatter_dimension=2, tiled=True)  153 us
    reduce_scatter x1, waiting for transfers between devices, body(): lax.psum_scatter(gate_part, 'ctx', scatter_dimension=1, tiled=True)  153 us
    reduce_scatter x1, waiting for transfers between devices, body(): lax.psum_scatter(up_part, 'ctx', scatter_dimension=1, tiled=True)  153 us
    reduce_scatter x1, waiting for transfers between devices, body(): lax.psum_scatter(o_part, 'ctx', scatter_dimension=1, tiled=True)  67.3 us
    reduce_scatter x1, waiting for transfers between devices, body(): lax.psum_scatter(q_part, 'ctx', scatter_dimension=0, tiled=True)  66.5 us
    reduce_scatter x1, waiting for transfers between devices, body(): lax.psum_scatter(k_part, 'ctx', scatter_dimension=0, tiled=True)  65 us
    reduce_scatter x1, waiting for transfers between devices, body(): lax.psum_scatter(v_part, 'ctx', scatter_dimension=0, tiled=True)  64.9 us
    reduce_scatter x1, waiting for transfers between devices, body(): lax.psum_scatter(d_key_term, 'ctx', scatter_dimension=0, tiled=True)  64.4 us
  transfers between devices with their start and end apart: 14, of which 14 were waited for; matrix products, arithmetic and copies ran while one was open for 4% of the time, Pallas kernels for 0%

commit v1 on v0

--- a/solution.py
+++ b/solution.py
@@ -8,6 +8,16 @@
 CAP = 112
 NORM_EPS = 1e-06
 ROPE_BASE = 10000.0
+
+
+def gather_by_hops(value, name, d):
+    size = lax.axis_size(name)
+    held, blocks = (value, [value])
+    for _ in range(size - 1):
+        held = lax.ppermute(held, name, [(i, (i + 1) % size) for i in range(size)])
+        blocks.insert(0, held)
+    line = jnp.concatenate(blocks, axis=d)
+    return jnp.roll(line, (lax.axis_index(name) + 1) * value.shape[d], axis=d)
 
 
 def rope_tables(positions, head_width):
@@ -152,7 +162,7 @@
     new_top = jnp.maximum(running_top, jnp.max(scores, axis=-1))
     new_total = jnp.sum(jnp.exp(scores - new_top[..., None]), axis=-1)
     log_total = new_top + jnp.log(new_total)
-    key_piece = lax.all_gather(key_rot, "ctx", axis=0, tiled=True)
+    key_piece = gather_by_hops(key_rot, "ctx", 0)
     value_piece = lax.all_gather(value_proj, "ctx", axis=0, tiled=True)
     scores = masked_scores(key_piece, jnp.int32(0))
     probs = jnp.exp(scores - log_total[..., None]).astype(jnp.bfloat16)

time: 1200 us -> 1230 us (1.025)
  waiting for transfers between devices: 975 us -> 1010 us
    ppermute x0 -> x7, waiting for transfers between devices: none -> 32.3 us  [gather_by_hops(): held = lax.ppermute(held, name, [(i, (i + 1) % size) for i in range(size)])]
  transfers between devices with their start and end apart: 14 -> 21, of which waited for: 14 -> 19; matrix products, arithmetic and copies ran while one was open for 4% -> 4% of each run, Pallas kernels for 0% -> 0%
where the time goes in v1:
time: 1230 us
  waiting for transfers between devices  1010 us (82%)
  blocking collectives  85.7 us (7%)
  matrix products  46.4 us (4%)
  local copies, waits for them, and re-layouts  45 us (4%)
  other arithmetic  25.5 us (2%)
  between operations  15.5 us (1%)
    reduce_scatter x1, waiting for transfers between devices, body(): lax.psum_scatter(gate_part, 'ctx', scatter_dimension=1, tiled=True)  153 us
    reduce_scatter x1, waiting for transfers between devices, body(): lax.psum_scatter(down_part, 'ctx', scatter_dimension=2, tiled=True)  153 us
    reduce_scatter x1, waiting for transfers between devices, body(): lax.psum_scatter(up_part, 'ctx', scatter_dimension=1, tiled=True)  153 us
    reduce_scatter x1, waiting for transfers between devices, body(): lax.psum_scatter(o_part, 'ctx', scatter_dimension=1, tiled=True)  67.3 us
    reduce_scatter x1, waiting for transfers between devices, body(): lax.psum_scatter(q_part, 'ctx', scatter_dimension=0, tiled=True)  66.5 us
    reduce_scatter x1, waiting for transfers between devices, body(): lax.psum_scatter(k_part, 'ctx', scatter_dimension=0, tiled=True)  65.1 us
    reduce_scatter x1, waiting for transfers between devices, body(): lax.psum_scatter(v_part, 'ctx', scatter_dimension=0, tiled=True)  64.9 us
    reduce_scatter x1, waiting for transfers between devices, body(): lax.psum_scatter(d_key_term, 'ctx', scatter_dimension=0, tiled=True)  63.9 us
  transfers between devices with their start and end apart: 21, of which 19 were waited for; matrix products, arithmetic and copies ran while one was open for 4% of the time, Pallas kernels for 0%

profile of v1, /device:TPU:0, one launch (start us, length us, event | category | flops | bytes accessed | tf_op | source)
XLA Modules:
  0.0 1232.6 jit_solution(16448266215680698728)
XLA Ops:
  13.1 26.9 %all_gather.8 = bf16[1024,128]{0,1:T(8,128)(2,1)S(1)} all-gather(bf16[128,128]{0,1:T(8,128)(2,1)S(1)} %fusion.57), channel_id=1, replica_groups=mesh['ctx'=8,'shard'=4] {'ctx'}, dimensions={0}, use_global_device_ids=true | all-gather | bytes 294912 | tf_op jit(solution)/shard_map/all_gather | solution.py:161
  43.3 6.5 collective-permute-done.1
  56.4 6.5 collective-permute-done.3
  63.0 6.5 collective-permute-done.4
  69.7 6.5 collective-permute-done.5
  76.2 30.7 %all_gather.9 = bf16[1024,128]{1,0:T(8,128)(2,1)S(1)} all-gather(bf16[128,128]{1,0:T(8,128)(2,1)S(1)} %convolution_convert_fusion.1), channel_id=1, replica_groups=mesh['ctx'=8,'shard'=4] {'ctx'}, dimensions={0}, use_global_device_ids=true | all-gather | bytes 294912 | tf_op jit(solution)/shard_map/all_gather | solution.py:166
  109.8 7.1 gather_fusion.5
  120.4 23.7 %all-reduce.8.cloned.1.call-done = f32[128,1024]{1,0:T(8,128)} async-done(((f32[128,1024]{1,0:T(8,128)}), f32[128,1024]{1,0:T(8,128)}) %all-reduce.8.cloned.1.call-update) | async-done | bytes 524304 | tf_op jit(solution)/shard_map/psum | solution.py:179
  148.5 7.0 gather_fusion.4
  177.5 6.4 psum.38
  206.8 32.4 %all-reduce.12.cloned.1.call-done = f32[128,1024]{1,0:T(8,128)} async-done(((f32[128,1024]{1,0:T(8,128)}), f32[128,1024]{1,0:T(8,128)}) %all-reduce.12.cloned.1.call-update) | async-done | bytes 524304 | tf_op jit(solution)/shard_map/psum | solution.py:227
  241.6 32.0 %all-reduce.10.cloned.1.call-done = bf16[128,1024]{1,0:T(8,128)(2,1)} async-done(((bf16[128,1024]{1,0:T(8,128)(2,1)}), bf16[128,1024]{1,0:T(8,128)(2,1)}) %all-reduce.10.cloned.1.call-update) | async-done | bytes 262160 | tf_op jit(solution)/shard_map/psum | solution.py:205
  281.9 63.9 %reduce-scatter.11.cloned.1.call-done = f32[128,128]{0,1:T(8,128)} async-done(((f32[1024,128]{0,1:T(8,128)}), f32[128,128]{0,1:T(8,128)}) %reduce-scatter.11.cloned.1.call-update) | async-done | bytes 65552 | tf_op jit(solution)/shard_map/reduce_scatter | solution.py:292
  347.8 63.2 %reduce-scatter.13.cloned.1.call-done = f32[128,128]{0,1:T(8,128)} async-done(((f32[1024,128]{0,1:T(8,128)}), f32[128,128]{0,1:T(8,128)}) %reduce-scatter.13.cloned.1.call-update) | async-done | bytes 65552 | tf_op jit(solution)/shard_map/reduce_scatter | solution.py:293
  438.6 7.5 all-reduce.14.cloned.1.call-done
  447.3 21.6 %all-reduce.2 = (f32[1024]{0:T(1024)S(1)}, f32[1024]{0:T(1024)S(1)}) all-reduce(f32[1024]{0:T(1024)S(1)} %get-tuple-element.184, f32[1024]{0:T(1024)S(1)} %get-tuple-element.182), channel_id=4, replica_groups=mesh['ctx'=8,'shard'=4] {'ctx'}, use_global_device_ids=true, to_apply=%region_30.31.clone | all-reduce | flops 2048 | bytes 16384
  472.2 31.6 %reduce-scatter.23.cloned.1.call-done = f32[128,16]{0,1:T(8,128)} async-done(((f32[1024,16]{0,1:T(8,128)}), f32[128,16]{0,1:T(8,128)}) %reduce-scatter.23.cloned.1.call-update) | async-done | bytes 8208 | tf_op jit(solution)/shard_map/reduce_scatter | solution.py:335
  503.8 67.3 %reduce-scatter.21.cloned.1.call-done = f32[256,128]{1,0:T(8,128)} async-done(((f32[256,1024]{1,0:T(8,128)}), f32[256,128]{1,0:T(8,128)}) %reduce-scatter.21.cloned.1.call-update) | async-done | bytes 131088 | tf_op jit(solution)/shard_map/reduce_scatter | solution.py:333
  571.1 64.9 %reduce-scatter.19.cloned.1.call-done = f32[128,128]{1,0:T(8,128)} async-done(((f32[1024,128]{1,0:T(8,128)}), f32[128,128]{1,0:T(8,128)}) %reduce-scatter.19.cloned.1.call-update) | async-done | bytes 65552 | tf_op jit(solution)/shard_map/reduce_scatter | solution.py:332
  636.0 65.1 %reduce-scatter.17.cloned.1.call-done = f32[128,128]{1,0:T(8,128)} async-done(((f32[1024,128]{1,0:T(8,128)}), f32[128,128]{1,0:T(8,128)}) %reduce-scatter.17.cloned.1.call-update) | async-done | bytes 65552 | tf_op jit(solution)/shard_map/reduce_scatter | solution.py:331
  701.1 66.5 %reduce-scatter.15.cloned.1.call-done = f32[128,256]{1,0:T(8,128)} async-done(((f32[1024,256]{1,0:T(8,128)}), f32[128,256]{1,0:T(8,128)}) %reduce-scatter.15.cloned.1.call-update) | async-done | bytes 131088 | tf_op jit(solution)/shard_map/reduce_scatter | solution.py:330
  767.6 152.9 %reduce-scatter.29.cloned.1.call-done = f32[4,512,128]{2,1,0:T(8,128)} async-done(((f32[4,512,1024]{2,1,0:T(8,128)}), f32[4,512,128]{2,1,0:T(8,128)}) %reduce-scatter.29.cloned.1.call-update) | async-done | bytes 1048592 | tf_op jit(solution)/shard_map/reduce_scatter | solution.py:338
  920.5 152.6 %reduce-scatter.27.cloned.1.call-done = f32[4,128,512]{2,1,0:T(8,128)} async-done(((f32[4,1024,512]{2,1,0:T(8,128)}), f32[4,128,512]{2,1,0:T(8,128)}) %reduce-scatter.27.cloned.1.call-update) | async-done | bytes 1048592 | tf_op jit(solution)/shard_map/reduce_scatter | solution.py:337
  1073.1 152.9 %reduce-scatter.25.cloned.1.call-done = f32[4,128,512]{2,1,0:T(8,128)} async-done(((f32[4,1024,512]{2,1,0:T(8,128)}), f32[4,128,512]{2,1,0:T(8,128)}) %reduce-scatter.25.cloned.1.call-update) | async-done | bytes 1048592 | tf_op jit(solution)/shard_map/reduce_scatter | solution.py:336
  (274 shorter events, 117.3 us)
Async XLA Ops:
  7.2 101.1 %copy-start = (bf16[256,1024]{1,0:T(8,128)(2,1)S(1)}, bf16[256,1024]{1,0:T(8,128)(2,1)}, u32[]{:S(2)}) copy-start(bf16[256,1024]{1,0:T(8,128)(2,1)} %param.20) | copy-start | bytes 1572868
  7.2 136.9 %all-reduce.8.cloned.1.call-start = ((), (), s32[]{:S(2)}) async-start(), calls=%async_computation.10 | async-start | bytes 1048576 | tf_op jit(solution)/shard_map/psum | solution.py:179
  10.1 33.0 %collective-permute-start = (bf16[128,128]{0,1:T(8,128)(2,1)S(1)}, bf16[128,128]{0,1:T(8,128)(2,1)S(1)}, u32[]{:S(2)}, u32[]{:S(2)}) collective-permute-start(bf16[128,128]{0,1:T(8,128)(2,1)S(1)} %fusion.57), channel_id=1, source_target_pairs={{0,4},{4,8},{8,12},{12,16},{16,20},{20,24},{24,28},{28,0},{1,5},{5... | collective-permute-start | bytes 98312 | tf_op jit(solution)/shard_map/ppermute | solution.py:17
  43.1 6.7 collective-permute-start.1
  49.7 6.6 collective-permute-start.2
  56.3 6.6 collective-permute-start.3
  63.0 6.6 collective-permute-start.4
  69.6 6.6 collective-permute-start.5
  76.2 30.9 %collective-permute-start.6 = (bf16[128,128]{0,1:T(8,128)(2,1)S(1)}, bf16[128,128]{0,1:T(8,128)(2,1)S(1)}, u32[]{:S(2)}, u32[]{:S(2)}) collective-permute-start(bf16[128,128]{0,1:T(8,128)(2,1)S(1)} %collective-permute-done.5), channel_id=1, source_target_pairs={{0,4},{4,8},{8,12},{12,16},{16,20},{20,24},{24,28},{28,0},{1,5},{5... | collective-permute-start | bytes 98312 | tf_op jit(solution)/shard_map/ppermute | solution.py:17
  109.4 129.8 %all-reduce.12.cloned.1.call-start = ((), (), s32[]{:S(2)}) async-start(), calls=%async_computation.12 | async-start | bytes 1048576 | tf_op jit(solution)/shard_map/psum | solution.py:227
  205.8 67.8 %all-reduce.10.cloned.1.call-start = ((), (), s32[]{:S(2)}) async-start(), calls=%async_computation.11 | async-start | bytes 524288 | tf_op jit(solution)/shard_map/psum | solution.py:205
  206.5 139.3 %reduce-scatter.11.cloned.1.call-start = ((), (), s32[]{:S(2)}) async-start(), calls=%async_computation.13 | async-start | bytes 589824 | tf_op jit(solution)/shard_map/reduce_scatter | solution.py:292
  280.6 66.9 %copy-start.27 = (bf16[1024,128]{1,0:T(8,128)(2,1)S(1)}, bf16[1024,128]{1,0:T(8,128)(2,1)}, u32[]{:S(2)}) copy-start(bf16[1024,128]{1,0:T(8,128)(2,1)} %param.18) | copy-start | bytes 786436
  280.6 130.4 %reduce-scatter.13.cloned.1.call-start = ((), (), s32[]{:S(2)}) async-start(), calls=%async_computation.14 | async-start | bytes 589824 | tf_op jit(solution)/shard_map/reduce_scatter | solution.py:293
  280.7 130.3 %copy-start.28 = (bf16[1024,128]{1,0:T(8,128)(2,1)S(1)}, bf16[1024,128]{1,0:T(8,128)(2,1)}, u32[]{:S(2)}) copy-start(bf16[1024,128]{1,0:T(8,128)(2,1)} %param.19) | copy-start | bytes 786436
  281.2 164.9 %all-reduce.14.cloned.1.call-start = ((), (), s32[]{:S(2)}) async-start(), calls=%async_computation.15 | async-start | bytes 1048576 | tf_op jit(solution)/shard_map/psum | solution.py:314
  412.9 90.9 %reduce-scatter.23.cloned.1.call-start = ((), (), s32[]{:S(2)}) async-start(), calls=%async_computation.20 | async-start | bytes 73728 | tf_op jit(solution)/shard_map/reduce_scatter | solution.py:335
  413.8 157.3 %reduce-scatter.21.cloned.1.call-start = ((), (), s32[]{:S(2)}) async-start(), calls=%async_computation.19 | async-start | bytes 1179648 | tf_op jit(solution)/shard_map/reduce_scatter | solution.py:333
  415.2 220.8 %reduce-scatter.19.cloned.1.call-start = ((), (), s32[]{:S(2)}) async-start(), calls=%async_computation.18 | async-start | bytes 589824 | tf_op jit(solution)/shard_map/reduce_scatter | solution.py:332
  416.4 284.6 %reduce-scatter.17.cloned.1.call-start = ((), (), s32[]{:S(2)}) async-start(), calls=%async_computation.17 | async-start | bytes 589824 | tf_op jit(solution)/shard_map/reduce_scatter | solution.py:331
  417.7 349.9 %reduce-scatter.15.cloned.1.call-start = ((), (), s32[]{:S(2)}) async-start(), calls=%async_computation.16 | async-start | bytes 1179648 | tf_op jit(solution)/shard_map/reduce_scatter | solution.py:330
  419.1 501.4 %reduce-scatter.29.cloned.1.call-start = ((), (), s32[]{:S(2)}) async-start(), calls=%async_computation.23 | async-start | bytes 9437184 | tf_op jit(solution)/shard_map/reduce_scatter | solution.py:338
  425.2 647.9 %reduce-scatter.27.cloned.1.call-start = ((), (), s32[]{:S(2)}) async-start(), calls=%async_computation.22 | async-start | bytes 9437184 | tf_op jit(solution)/shard_map/reduce_scatter | solution.py:337
  431.1 795.0 %reduce-scatter.25.cloned.1.call-start = ((), (), s32[]{:S(2)}) async-start(), calls=%async_computation.21 | async-start | bytes 9437184 | tf_op jit(solution)/shard_map/reduce_scatter | solution.py:336
  (46 other events, 667.0 us)
Sparse Core Ops, SparseCore 0:
  109.5 34.5 all-reduce.7
  205.9 33.2 all-reduce.11
  241.5 31.9 all-reduce.9
  280.7 65.0 reduce-scatter.10
  349.5 61.4 reduce-scatter.12
  413.9 32.1 all-reduce.13
  450.1 53.6 reduce-scatter.22
  508.2 62.8 reduce-scatter.20
  575.1 60.8 reduce-scatter.18
  640.1 60.9 reduce-scatter.16
  705.1 62.4 reduce-scatter.14
  772.1 148.3 reduce-scatter.28
  924.7 148.3 reduce-scatter.26
  1077.6 148.3 reduce-scatter.24
